TPU v7x, 32 devices: a whole 2x2x4 slice. The times are simulated.
32 devices in a mesh: pair: 8 (over z, x), col: 4 (over y, core).
Axes of the slice: x: 2, y: 2, z: 4, core: 2. Of those that a mesh axis runs over, the one named last changes fastest.
Arguments:
- point_values: bfloat16 [32768, 1024], P('pair', 'col'), may hold values from -2 to 2, as said below
- grid_values: bfloat16 [32768, 512], P('pair'), may hold values from -6 to 6
Outputs:
- fitted: float32 [512, 1024], P(('pair', 'col'))
Inputs may be any that keep to these rules, and one draw needn't show every extreme that they name: `point_values`: real pair-product values.
All inputs are finite; a program needn't handle non-finite values.
Results may differ from a plain program's by a relative error of at most 0.0003.
Values may be sent and summed in bfloat16 or wider, within the bound.
A program may use at most 128 MiB of HBM per device.

v0:
```python
import jax
import jax.numpy as jnp
from jax import lax
from jax.sharding import PartitionSpec as P


def cross(left, right):
    return lax.dot_general(
        left, right, (((0,), (0,)), ((), ())), preferred_element_type=jnp.float32
    )


def body(point_values, grid_values):
    gathered = lax.all_gather(point_values, "col", axis=1, tiled=True)
    gram = lax.psum(cross(gathered, gathered), "pair")
    factor = jnp.linalg.cholesky(gram)
    summed = lax.psum_scatter(
        cross(grid_values, point_values), "pair", scatter_dimension=0, tiled=True
    )
    regrouped = lax.all_to_all(summed, "col", split_axis=0, concat_axis=1, tiled=True)
    solved = jax.scipy.linalg.cho_solve((factor, True), regrouped.T)
    return solved.T


def solution(mesh):
    in_specs = (P("pair", "col"), P("pair", None))
    out_specs = P(("pair", "col"), None)
    return jax.shard_map(body, mesh=mesh, in_specs=in_specs, out_specs=out_specs, check_vma=False)
```

profile of v0, /device:TPU:0, one launch (start us, length us, event | category | flops | bytes accessed | tf_op | source)
XLA Modules:
  0.0 594.1 jit_solution(14145770324071007327)
XLA Ops:
  8.1 5.0 fusion.96
  13.2 58.8 %all-gather.2.cloned.1.call-done = bf16[4096,1024]{1,0:T(8,128)(2,1)} async-done(((bf16[4096,256]{1,0:T(8,128)(2,1)}), bf16[4096,1024]{1,0:T(8,128)(2,1)}) %all-gather.2.cloned.1.call-update) | async-done | bytes 8388624 | tf_op jit(solution)/shard_map/all_gather | solution.py:14
  72.0 15.1 %fusion.95 = f32[1024,1024]{0,1:T(8,128)} fusion(bf16[4096,1024]{1,0:T(8,128)(2,1)} %all-gather.2.cloned.1.call-done), kind=kOutput, calls=%fused_computation.213 | convolution fusion | flops 8589934592 | bytes 12582912 | tf_op jit(solution)/shard_map/dot_general | solution.py:8
  87.1 3.3 all-to-all-start
  90.4 4.1 all-to-all-done
  94.5 148.8 %all-reduce.3.cloned.1.call-done = f32[1024,1024]{0,1:T(8,128)} async-done(((f32[1024,1024]{0,1:T(8,128)}), f32[1024,1024]{0,1:T(8,128)}) %all-reduce.3.cloned.1.call-update) | async-done | bytes 4194320 | tf_op jit(solution)/shard_map/psum | solution.py:15
  243.3 5.6 copy.9
  248.9 4.4 fusion
  253.4 1.9 copy-done
  255.3 11.7 %cholesky.223 = f32[128,128]{1,0:T(8,128)S(1)} custom-call(f32[128,128]{1,0:T(8,128)S(1)} %cholesky.580), custom_call_target="Cholesky" | custom-call | tf_op jit(solution)/shard_map/jit(cholesky)/cholesky | solution.py:16
  267.0 9.8 %custom-call.66 = f32[1,128,128]{1,2,0:T(8,128)S(1)} custom-call(f32[1,128,128]{2,1,0:T(8,128)S(1)} %get-tuple-element.44), custom_call_target="InvertDiagBlocksLowerTriangular" | custom-call | tf_op jit(solution)/shard_map/jit(cholesky)/cholesky | solution.py:16
  276.9 2.5 cholesky.255
  279.4 2.4 constant_dynamic-update-slice_fusion.50
  281.7 1.5 convolution_subtract_fusion
  283.3 12.2 %cholesky.244 = f32[128,128]{1,0:T(8,128)S(1)} custom-call(f32[128,128]{1,0:T(8,128)S(1)} %cholesky.584), custom_call_target="Cholesky" | custom-call | tf_op jit(solution)/shard_map/jit(cholesky)/cholesky | solution.py:16
  296.2 9.8 %custom-call.67 = f32[1,128,128]{1,2,0:T(8,128)S(1)} custom-call(f32[1,128,128]{2,1,0:T(8,128)S(1)} %get-tuple-element.41), custom_call_target="InvertDiagBlocksLowerTriangular" | custom-call | tf_op jit(solution)/shard_map/jit(cholesky)/cholesky | solution.py:16
  306.0 1.2 convolution_dynamic-update-slice_fusion
  307.2 2.1 convolution_subtract_fusion.1
  309.3 11.7 %cholesky.468 = f32[128,128]{1,0:T(8,128)S(1)} custom-call(f32[128,128]{1,0:T(8,128)S(1)} %cholesky.589), custom_call_target="Cholesky" | custom-call | tf_op jit(solution)/shard_map/jit(cholesky)/cholesky | solution.py:16
  322.3 9.8 %custom-call.68 = f32[1,128,128]{1,2,0:T(8,128)S(1)} custom-call(f32[1,128,128]{2,1,0:T(8,128)S(1)} %get-tuple-element.38), custom_call_target="InvertDiagBlocksLowerTriangular" | custom-call | tf_op jit(solution)/shard_map/jit(cholesky)/cholesky | solution.py:16
  332.1 1.2 convolution_dynamic-update-slice_fusion.1
  333.3 2.3 convolution_subtract_fusion.2
  335.6 11.8 %cholesky.487 = f32[128,128]{1,0:T(8,128)S(1)} custom-call(f32[128,128]{1,0:T(8,128)S(1)} %cholesky.594), custom_call_target="Cholesky" | custom-call | tf_op jit(solution)/shard_map/jit(cholesky)/cholesky | solution.py:16
  348.8 9.8 %custom-call.69 = f32[1,128,128]{1,2,0:T(8,128)S(1)} custom-call(f32[1,128,128]{2,1,0:T(8,128)S(1)} %get-tuple-element.35), custom_call_target="InvertDiagBlocksLowerTriangular" | custom-call | tf_op jit(solution)/shard_map/jit(cholesky)/cholesky | solution.py:16
  358.6 1.1 convolution_dynamic-update-slice_fusion.2
  359.7 2.3 convolution_subtract_fusion.3
  362.0 11.7 %cholesky.506 = f32[128,128]{1,0:T(8,128)S(1)} custom-call(f32[128,128]{1,0:T(8,128)S(1)} %cholesky.599), custom_call_target="Cholesky" | custom-call | tf_op jit(solution)/shard_map/jit(cholesky)/cholesky | solution.py:16
  375.0 10.0 %custom-call.70 = f32[1,128,128]{1,2,0:T(8,128)S(1)} custom-call(f32[1,128,128]{2,1,0:T(8,128)S(1)} %get-tuple-element.32), custom_call_target="InvertDiagBlocksLowerTriangular" | custom-call | tf_op jit(solution)/shard_map/jit(cholesky)/cholesky | solution.py:16
  385.0 1.0 convolution_dynamic-update-slice_fusion.3
  386.0 2.3 convolution_subtract_fusion.4
  388.3 11.7 %cholesky.526 = f32[128,128]{1,0:T(8,128)S(1)} custom-call(f32[128,128]{1,0:T(8,128)S(1)} %cholesky.604), custom_call_target="Cholesky" | custom-call | tf_op jit(solution)/shard_map/jit(cholesky)/cholesky | solution.py:16
  401.3 9.8 %custom-call.71 = f32[1,128,128]{1,2,0:T(8,128)S(1)} custom-call(f32[1,128,128]{2,1,0:T(8,128)S(1)} %get-tuple-element.29), custom_call_target="InvertDiagBlocksLowerTriangular" | custom-call | tf_op jit(solution)/shard_map/jit(cholesky)/cholesky | solution.py:16
  411.1 0.9 convolution_dynamic-update-slice_fusion.4
  412.1 2.0 convolution_subtract_fusion.5
  414.1 12.1 %cholesky.546 = f32[128,128]{1,0:T(8,128)S(1)} custom-call(f32[128,128]{1,0:T(8,128)S(1)} %cholesky.609), custom_call_target="Cholesky" | custom-call | tf_op jit(solution)/shard_map/jit(cholesky)/cholesky | solution.py:16
  427.5 9.8 %custom-call.72 = f32[1,128,128]{1,2,0:T(8,128)S(1)} custom-call(f32[1,128,128]{2,1,0:T(8,128)S(1)} %get-tuple-element.26), custom_call_target="InvertDiagBlocksLowerTriangular" | custom-call | tf_op jit(solution)/shard_map/jit(cholesky)/cholesky | solution.py:16
  437.3 0.8 convolution_dynamic-update-slice_fusion.5
  438.1 1.8 convolution_subtract_fusion.6
  439.9 11.7 %cholesky.564 = f32[128,128]{1,0:T(8,128)S(1)} custom-call(f32[128,128]{1,0:T(8,128)S(1)} %convolution_subtract_fusion.6), custom_call_target="Cholesky" | custom-call | tf_op jit(solution)/shard_map/jit(cholesky)/cholesky | solution.py:16
  458.5 4.8 select_select_fusion
  463.2 22.8 %while.1 = (s32[]{:T(128)}, f32[1024,1024]{1,0:T(8,128)}, s32[8,2]{0,1:T(2,128)S(1)}, f32[8,128,128]{2,1,0:T(8,128)S(1)}, s32[]{:T(128)}) while((s32[]{:T(128)}, f32[1024,1024]{1,0:T(8,128)}, s32[8,2]{0,1:T(2,128)S(1)}, f32[8,128,128]{2,1,0:T(8,128)S(1)}, s32[]{:T(128)}) %tuple.56), condition=%wide.while_cond, body=%wide.while_body.sunk | while | flops 2 | bytes 131181 | solution.py:21
  463.9 2.2 bitcast_dynamic-update-slice_fusion.2
  466.7 2.2 bitcast_dynamic-update-slice_fusion.2
  469.6 2.2 bitcast_dynamic-update-slice_fusion.2
  472.5 2.2 bitcast_dynamic-update-slice_fusion.2
  475.3 2.2 bitcast_dynamic-update-slice_fusion.2
  478.2 2.2 bitcast_dynamic-update-slice_fusion.2
  481.1 2.2 bitcast_dynamic-update-slice_fusion.2
  483.9 2.2 bitcast_dynamic-update-slice_fusion.2
  486.1 78.8 %custom-call.73 = f32[8,128,128]{1,2,0:T(8,128)S(1)} custom-call(f32[8,128,128]{2,1,0:T(8,128)S(1)} %get-tuple-element.12), custom_call_target="InvertDiagBlocksLowerTriangular" | custom-call | tf_op jit(solution)/shard_map/jit(_cho_solve)/triangular_solve | solution.py:21
  565.0 1.0 convolution_subtract_fusion.14
  566.3 1.1 convolution_subtract_fusion.13
  567.6 1.3 convolution_subtract_fusion.12
  569.0 1.2 convolution_subtract_fusion.11
  570.4 1.4 convolution_subtract_fusion.20
  572.0 1.4 convolution_subtract_fusion.19
  573.6 1.6 convolution_subtract_fusion.18
  575.5 1.0 convolution_subtract_fusion.10
  576.8 1.1 convolution_subtract_fusion.9
  578.1 1.2 convolution_subtract_fusion.8
  579.5 1.2 convolution_subtract_fusion.7
  581.0 1.3 convolution_subtract_fusion.17
  582.6 1.3 convolution_subtract_fusion.16
  584.2 1.4 convolution_subtract_fusion.15
  (90 shorter events, 18.8 us)
Async XLA Ops:
  7.4 64.6 %all-gather.2.cloned.1.call-start = ((), (), s32[]{:S(2)}) async-start(), calls=%async_computation.2 | async-start | bytes 10485760 | tf_op jit(solution)/shard_map/all_gather | solution.py:14
  8.1 79.0 %reduce-scatter.2.cloned.1.call-start = ((), (), s32[]{:S(2)}) async-start(), calls=%async_computation.4 | async-start | bytes 589824 | tf_op jit(solution)/shard_map/reduce_scatter | solution.py:17
  13.1 230.2 %all-reduce.3.cloned.1.call-start = ((), (), s32[]{:S(2)}) async-start(), calls=%async_computation.3 | async-start | bytes 8388608 | tf_op jit(solution)/shard_map/psum | solution.py:15
  87.1 7.4 %all-to-all-start = ((f32[4,16,256]{2,1,0:T(8,128)}), f32[4,16,256]{2,1,0:T(8,128)S(1)}, u32[]{:S(2)}, u32[]{:S(2)}) async-start(f32[4,16,256]{2,1,0:T(8,128)} %bitcast.147), calls=%async_computation.1 | async-start | bytes 131072 | tf_op jit(solution)/shard_map/all_to_all | solution.py:20
  253.4 1.9 copy-start
  585.8 0.6 copy-start.1
Sparse Core Ops, SparseCore 0:
  9.8 62.1 all-gather.1
Sparse Core Ops, SparseCore 1:
  13.2 64.7 reduce-scatter.1
  87.2 156.1 all-reduce.2
where the time goes:
time: 600 us; the launch traced here: 594 us
  other arithmetic  261 us (44%)
  waiting for transfers between devices  212 us (35%)
  matrix products  63.6 us (11%)
  local copies, waits for them, and re-layouts  33.6 us (6%)
  between operations  20.3 us (3%)
    another operation x30, other arithmetic, body(): factor = jnp.linalg.cholesky(gram)  173 us
    psum x1, waiting for transfers between devices, body(): gram = lax.psum(cross(gathered, gathered), 'pair')  149 us
    another operation x3, other arithmetic, body(): solved = jax.scipy.linalg.cho_solve((factor, True), regrouped.T)  83.6 us
    all_gather x1, waiting for transfers between devices, body(): gathered = lax.all_gather(point_values, 'col', axis=1, tiled=True)  58.8 us
    another operation x14, matrix products, body(): factor = jnp.linalg.cholesky(gram)  23.1 us
    another operation x24, local copies, waits for them, and re-layouts  22.7 us
    another operation x30, matrix products, body(): solved = jax.scipy.linalg.cho_solve((factor, True), regrouped.T)  20.5 us
    dot_general x2, matrix products, cross(): lax.dot_general(left, right, (((0,), (0,)), ((), ())), preferred_element_...  20 us
  transfers between devices with their start and end apart: 4, of which 3 were waited for; matrix products, arithmetic and copies ran while one was open for 3% of the time, Pallas kernels for 0%

commit v1 on v0

--- a/solution.py
+++ b/solution.py
@@ -11,7 +11,21 @@
 
 
 def body(point_values, grid_values):
-    gathered = lax.all_gather(point_values, "col", axis=1, tiled=True)
+    ways, here, step = (lax.axis_size("col"), lax.axis_index("col"), point_values.shape[1])
+    dims = [n * ways if d == 1 else n for d, n in enumerate(point_values.shape)]
+    full = lax.dynamic_update_slice_in_dim(
+        jnp.zeros(dims, point_values.dtype), point_values, here * step, axis=1
+    )
+    going_up = going_down = point_values
+    for far in range(1, ways // 2 + 1):
+        going_up = lax.ppermute(going_up, "col", [(d, (d + 1) % ways) for d in range(ways)])
+        full = lax.dynamic_update_slice_in_dim(full, going_up, (here - far) % ways * step, axis=1)
+        if 2 * far < ways:
+            going_down = lax.ppermute(going_down, "col", [(d, (d - 1) % ways) for d in range(ways)])
+            full = lax.dynamic_update_slice_in_dim(
+                full, going_down, (here + far) % ways * step, axis=1
+            )
+    gathered = full
     gram = lax.psum(cross(gathered, gathered), "pair")
     factor = jnp.linalg.cholesky(gram)
     summed = lax.psum_scatter(

time: 600 us -> 641 us (1.068)
  waiting for transfers between devices: 212 us -> 247 us
    all_gather x1 -> x0, waiting for transfers between devices: 58.8 us -> none  [body(): gathered = lax.all_gather(point_values, 'col', axis=1, tiled=True)]
    ppermute x0 -> x3, waiting for transfers between devices: none -> 57.2 us  [the longest x2 57.2 us: body(): lax.ppermute(going_up, 'col', [(d, (d + 1) % ways) for d in range(ways)])]
    reduce_scatter x1, waiting for transfers between devices: 0.03 us -> 33.1 us  [body(): lax.psum_scatter(cross(grid_values, point_values), 'pair', scatter_dimens...]
  transfers between devices with their start and end apart: 4 -> 6, of which waited for: 3 -> 5; matrix products, arithmetic and copies ran while one was open for 3% -> 3% of each run, Pallas kernels for 0% -> 0%
where the time goes in v1:
time: 641 us; the launch traced here: 634 us
  other arithmetic  260 us (41%)
  waiting for transfers between devices  247 us (39%)
  matrix products  59.3 us (9%)
  local copies, waits for them, and re-layouts  39.9 us (6%)
  between operations  19 us (3%)
  starting transfers between devices  8.42 us (1%)
    another operation x30, other arithmetic, body(): factor = jnp.linalg.cholesky(gram)  172 us
    psum x1, waiting for transfers between devices, body(): gram = lax.psum(cross(gathered, gathered), 'pair')  152 us
    another operation x3, other arithmetic, body(): solved = jax.scipy.linalg.cho_solve((factor, True), regrouped.T)  83.6 us
    ppermute x2, waiting for transfers between devices, body(): lax.ppermute(going_up, 'col', [(d, (d + 1) % ways) for d in range(ways)])  57.2 us
    reduce_scatter x1, waiting for transfers between devices, body(): lax.psum_scatter(cross(grid_values, point_values), 'pair', scatter_dimens...  33.1 us
    another operation x14, matrix products, body(): factor = jnp.linalg.cholesky(gram)  23.1 us
    another operation x24, local copies, waits for them, and re-layouts  22.7 us
    another operation x30, matrix products, body(): solved = jax.scipy.linalg.cho_solve((factor, True), regrouped.T)  20.5 us
  transfers between devices with their start and end apart: 6, of which 5 were waited for; matrix products, arithmetic and copies ran while one was open for 3% of the time, Pallas kernels for 0%

profile of v1, /device:TPU:0, one launch (start us, length us, event | category | flops | bytes accessed | tf_op | source)
XLA Modules:
  0.0 633.6 jit_solution(1009935115050659848)
XLA Ops:
  7.0 2.0 collective-permute-start.1
  8.9 43.7 %collective-permute-done = bf16[4096,256]{1,0:T(8,128)(2,1)S(1)} collective-permute-done((bf16[4096,256]{1,0:T(8,128)(2,1)}, bf16[4096,256]{1,0:T(8,128)(2,1)S(1)}, u32[]{:S(2)}, u32[]{:S(2)}) %collective-permute-start) | collective-permute-done | bytes 2097184 | tf_op jit(solution)/shard_map/ppermute | solution.py:21
  52.7 2.7 collective-permute-start.2
  55.4 5.0 fusion.113
  62.8 1.9 constant_dynamic-update-slice_fusion.45
  64.8 13.5 %collective-permute-done.2 = bf16[4096,256]{1,0:T(8,128)(2,1)} collective-permute-done((bf16[4096,256]{1,0:T(8,128)(2,1)S(1)}, bf16[4096,256]{1,0:T(8,128)(2,1)}, u32[]{:S(2)}, u32[]{:S(2)}) %collective-permute-start.2) | collective-permute-done | bytes 2097184 | tf_op jit(solution)/shard_map/ppermute | solution.py:21
  78.2 1.9 constant_dynamic-update-slice_fusion.44
  80.2 10.6 %fusion.112 = f32[1024,1024]{0,1:T(8,128)} fusion(bf16[4096,1024]{1,0:T(8,128)(2,1)S(1)} %constant_dynamic-update-slice_fusion.44), kind=kOutput, calls=%fused_computation.224 | convolution fusion | flops 8589934592 | bytes 12582912 | tf_op jit(solution)/shard_map/dot_general | solution.py:8
  90.8 33.1 %reduce-scatter.2.cloned.1.call-done = f32[64,256]{1,0:T(8,128)} async-done(((f32[512,256]{1,0:T(8,128)}), f32[64,256]{1,0:T(8,128)}) %reduce-scatter.2.cloned.1.call-update) | async-done | bytes 65552 | tf_op jit(solution)/shard_map/reduce_scatter | solution.py:31
  124.0 3.3 all-to-all-start
  127.3 4.1 all-to-all-done
  131.4 152.2 %all-reduce.3.cloned.1.call-done = f32[1024,1024]{0,1:T(8,128)} async-done(((f32[1024,1024]{0,1:T(8,128)}), f32[1024,1024]{0,1:T(8,128)}) %all-reduce.3.cloned.1.call-update) | async-done | bytes 4194320 | tf_op jit(solution)/shard_map/psum | solution.py:29
  283.5 5.8 copy.9
  289.3 4.4 fusion
  293.8 1.9 copy-done
  295.7 11.7 %cholesky.223 = f32[128,128]{1,0:T(8,128)S(1)} custom-call(f32[128,128]{1,0:T(8,128)S(1)} %cholesky.580), custom_call_target="Cholesky" | custom-call | tf_op jit(solution)/shard_map/jit(cholesky)/cholesky | solution.py:30
  307.4 2.5 cholesky.255
  309.9 9.8 %custom-call.66 = f32[1,128,128]{1,2,0:T(8,128)S(1)} custom-call(f32[1,128,128]{2,1,0:T(8,128)S(1)} %get-tuple-element.44), custom_call_target="InvertDiagBlocksLowerTriangular" | custom-call | tf_op jit(solution)/shard_map/jit(cholesky)/cholesky | solution.py:30
  319.8 2.4 constant_dynamic-update-slice_fusion.43
  322.1 1.5 slice_subtract_fusion
  323.7 11.9 %cholesky.244 = f32[128,128]{1,0:T(8,128)S(1)} custom-call(f32[128,128]{1,0:T(8,128)S(1)} %cholesky.584), custom_call_target="Cholesky" | custom-call | tf_op jit(solution)/shard_map/jit(cholesky)/cholesky | solution.py:30
  336.2 9.8 %custom-call.67 = f32[1,128,128]{1,2,0:T(8,128)S(1)} custom-call(f32[1,128,128]{2,1,0:T(8,128)S(1)} %get-tuple-element.41), custom_call_target="InvertDiagBlocksLowerTriangular" | custom-call | tf_op jit(solution)/shard_map/jit(cholesky)/cholesky | solution.py:30
  346.0 1.2 convolution_dynamic-update-slice_fusion
  347.3 2.1 slice_subtract_fusion.1
  349.4 11.7 %cholesky.468 = f32[128,128]{1,0:T(8,128)S(1)} custom-call(f32[128,128]{1,0:T(8,128)S(1)} %cholesky.589), custom_call_target="Cholesky" | custom-call | tf_op jit(solution)/shard_map/jit(cholesky)/cholesky | solution.py:30
  362.3 9.8 %custom-call.68 = f32[1,128,128]{1,2,0:T(8,128)S(1)} custom-call(f32[1,128,128]{2,1,0:T(8,128)S(1)} %get-tuple-element.38), custom_call_target="InvertDiagBlocksLowerTriangular" | custom-call | tf_op jit(solution)/shard_map/jit(cholesky)/cholesky | solution.py:30
  372.1 1.2 convolution_dynamic-update-slice_fusion.1
  373.3 2.3 slice_subtract_fusion.2
  375.7 11.9 %cholesky.487 = f32[128,128]{1,0:T(8,128)S(1)} custom-call(f32[128,128]{1,0:T(8,128)S(1)} %cholesky.594), custom_call_target="Cholesky" | custom-call | tf_op jit(solution)/shard_map/jit(cholesky)/cholesky | solution.py:30
  388.9 9.8 %custom-call.69 = f32[1,128,128]{1,2,0:T(8,128)S(1)} custom-call(f32[1,128,128]{2,1,0:T(8,128)S(1)} %get-tuple-element.35), custom_call_target="InvertDiagBlocksLowerTriangular" | custom-call | tf_op jit(solution)/shard_map/jit(cholesky)/cholesky | solution.py:30
  398.7 1.1 convolution_dynamic-update-slice_fusion.2
  399.8 2.3 slice_subtract_fusion.3
  402.1 11.7 %cholesky.506 = f32[128,128]{1,0:T(8,128)S(1)} custom-call(f32[128,128]{1,0:T(8,128)S(1)} %cholesky.599), custom_call_target="Cholesky" | custom-call | tf_op jit(solution)/shard_map/jit(cholesky)/cholesky | solution.py:30
  415.1 10.2 %custom-call.70 = f32[1,128,128]{1,2,0:T(8,128)S(1)} custom-call(f32[1,128,128]{2,1,0:T(8,128)S(1)} %get-tuple-element.32), custom_call_target="InvertDiagBlocksLowerTriangular" | custom-call | tf_op jit(solution)/shard_map/jit(cholesky)/cholesky | solution.py:30
  426.3 2.3 slice_subtract_fusion.4
  428.6 11.7 %cholesky.526 = f32[128,128]{1,0:T(8,128)S(1)} custom-call(f32[128,128]{1,0:T(8,128)S(1)} %cholesky.604), custom_call_target="Cholesky" | custom-call | tf_op jit(solution)/shard_map/jit(cholesky)/cholesky | solution.py:30
  441.6 9.8 %custom-call.71 = f32[1,128,128]{1,2,0:T(8,128)S(1)} custom-call(f32[1,128,128]{2,1,0:T(8,128)S(1)} %get-tuple-element.29), custom_call_target="InvertDiagBlocksLowerTriangular" | custom-call | tf_op jit(solution)/shard_map/jit(cholesky)/cholesky | solution.py:30
  452.4 2.0 slice_subtract_fusion.5
  454.4 11.9 %cholesky.546 = f32[128,128]{1,0:T(8,128)S(1)} custom-call(f32[128,128]{1,0:T(8,128)S(1)} %cholesky.609), custom_call_target="Cholesky" | custom-call | tf_op jit(solution)/shard_map/jit(cholesky)/cholesky | solution.py:30
  467.5 9.8 %custom-call.72 = f32[1,128,128]{1,2,0:T(8,128)S(1)} custom-call(f32[1,128,128]{2,1,0:T(8,128)S(1)} %get-tuple-element.26), custom_call_target="InvertDiagBlocksLowerTriangular" | custom-call | tf_op jit(solution)/shard_map/jit(cholesky)/cholesky | solution.py:30
  478.2 1.8 slice_subtract_fusion.6
  479.9 11.7 %cholesky.564 = f32[128,128]{1,0:T(8,128)S(1)} custom-call(f32[128,128]{1,0:T(8,128)S(1)} %slice_subtract_fusion.6), custom_call_target="Cholesky" | custom-call | tf_op jit(solution)/shard_map/jit(cholesky)/cholesky | solution.py:30
  498.5 4.8 select_select_fusion
  503.3 22.8 %while.1 = (s32[]{:T(128)}, f32[1024,1024]{1,0:T(8,128)}, s32[8,2]{0,1:T(2,128)S(1)}, f32[8,128,128]{2,1,0:T(8,128)S(1)}, s32[]{:T(128)}) while((s32[]{:T(128)}, f32[1024,1024]{1,0:T(8,128)}, s32[8,2]{0,1:T(2,128)S(1)}, f32[8,128,128]{2,1,0:T(8,128)S(1)}, s32[]{:T(128)}) %tuple.56), condition=%wide.while_cond, body=%wide.while_body.sunk | while | flops 2 | bytes 131181 | solution.py:35
  503.9 2.2 bitcast_dynamic-update-slice_fusion.2
  506.8 2.2 bitcast_dynamic-update-slice_fusion.2
  509.7 2.2 bitcast_dynamic-update-slice_fusion.2
  512.5 2.2 bitcast_dynamic-update-slice_fusion.2
  515.4 2.2 bitcast_dynamic-update-slice_fusion.2
  518.2 2.2 bitcast_dynamic-update-slice_fusion.2
  521.1 2.2 bitcast_dynamic-update-slice_fusion.2
  524.0 2.2 bitcast_dynamic-update-slice_fusion.2
  526.1 78.8 %custom-call.73 = f32[8,128,128]{1,2,0:T(8,128)S(1)} custom-call(f32[8,128,128]{2,1,0:T(8,128)S(1)} %get-tuple-element.12), custom_call_target="InvertDiagBlocksLowerTriangular" | custom-call | tf_op jit(solution)/shard_map/jit(_cho_solve)/triangular_solve | solution.py:35
  607.7 1.3 convolution_subtract_fusion.5
  609.1 1.2 convolution_subtract_fusion.4
  610.5 1.4 convolution_subtract_fusion.13
  612.1 1.4 convolution_subtract_fusion.12
  613.7 1.6 convolution_subtract_fusion.11
  616.9 1.1 convolution_subtract_fusion.2
  618.2 1.2 convolution_subtract_fusion.1
  619.6 1.2 convolution_subtract_fusion
  621.1 1.3 convolution_subtract_fusion.10
  622.7 1.3 convolution_subtract_fusion.9
  624.2 1.4 convolution_subtract_fusion.8
  (100 shorter events, 26.7 us)
Async XLA Ops:
  6.5 117.4 %reduce-scatter.2.cloned.1.call-start = ((), (), s32[]{:S(2)}) async-start(), calls=%async_computation.3 | async-start | bytes 589824 | tf_op jit(solution)/shard_map/reduce_scatter | solution.py:31
  6.5 46.1 %collective-permute-start = (bf16[4096,256]{1,0:T(8,128)(2,1)}, bf16[4096,256]{1,0:T(8,128)(2,1)S(1)}, u32[]{:S(2)}, u32[]{:S(2)}) collective-permute-start(bf16[4096,256]{1,0:T(8,128)(2,1)} %param.2), channel_id=1, source_target_pairs={{0,1},{1,2},{2,3},{3,0},{4,5},{5,6},{6,7},{7,4},{8,9},{9,10},{10,1... | collective-permute-start | bytes 6291464 | tf_op jit(solution)/shard_map/ppermute | solution.py:21
  7.0 55.8 %collective-permute-start.1 = (bf16[4096,256]{1,0:T(8,128)(2,1)}, bf16[4096,256]{1,0:T(8,128)(2,1)}, u32[]{:S(2)}, u32[]{:S(2)}) collective-permute-start(bf16[4096,256]{1,0:T(8,128)(2,1)} %param.2), channel_id=1, source_target_pairs={{0,3},{1,0},{2,1},{3,2},{4,7},{5,4},{6,5},{7,6},{8,11},{9,8},{10,9... | collective-permute-start | bytes 6291464 | tf_op jit(solution)/shard_map/ppermute | solution.py:24
  52.7 25.6 %collective-permute-start.2 = (bf16[4096,256]{1,0:T(8,128)(2,1)S(1)}, bf16[4096,256]{1,0:T(8,128)(2,1)}, u32[]{:S(2)}, u32[]{:S(2)}) collective-permute-start(bf16[4096,256]{1,0:T(8,128)(2,1)S(1)} %collective-permute-done), channel_id=1, source_target_pairs={{0,1},{1,2},{2,3},{3,0},{4,5},{5,6},{6,7},{7,4},{8,9},{9,10},{10,1... | collective-permute-start | bytes 6291464 | tf_op jit(solution)/shard_map/ppermute | solution.py:21
  60.4 223.1 %all-reduce.3.cloned.1.call-start = ((), (), s32[]{:S(2)}) async-start(), calls=%async_computation.2 | async-start | bytes 8388608 | tf_op jit(solution)/shard_map/psum | solution.py:29
  60.5 1.6 copy-start.1
  124.0 7.4 %all-to-all-start = ((f32[4,16,256]{2,1,0:T(8,128)}), f32[4,16,256]{2,1,0:T(8,128)S(1)}, u32[]{:S(2)}, u32[]{:S(2)}) async-start(f32[4,16,256]{2,1,0:T(8,128)} %bitcast.147), calls=%async_computation.1 | async-start | bytes 131072 | tf_op jit(solution)/shard_map/all_to_all | solution.py:34
  293.8 1.9 copy-start
  625.9 0.6 copy-start.2
Sparse Core Ops, SparseCore 0:
  60.5 63.4 reduce-scatter.1
  128.1 155.3 all-reduce.2
